TPU v7x, 32 devices: a whole 2x2x4 slice. The times are simulated.
32 devices in a mesh: row: 4 (over y, x), col: 8 (over z, core).
Axes of the slice: x: 2, y: 2, z: 4, core: 2. Of those that a mesh axis runs over, the one named last changes fastest.
Arguments:
- left_panel: float32 [4096, 8192], P('col', 'row'), may hold values from -6 to 6
- right_panel: float32 [4096, 16384], P('row', 'col'), may hold values from -0.09375 to 0.09375
- arc_basis: float32 [4096, 256], replicated, as said below
- normal_block: float32 [8192, 16384], P('row', 'col'), may hold values from -6 to 6
Outputs:
- updated_block: float32 [8192, 16384], P('row', 'col')
- left_reduced: float32 [4096, 8192], P('col', 'row')
- right_reduced: float32 [4096, 16384], P('row', 'col')
Inputs may be any that keep to these rules, and one draw needn't show every extreme that they name: arc_basis has orthonormal columns: arc_basis^T arc_basis equals the 256 x 256 identity within float32 rounding.
All inputs are finite; a program needn't handle non-finite values.
Results may differ from a plain program's by a relative error of at most 0.00005.
Values sent between devices are 32-bit elements; how exact they have to be, the bound alone decides.
A program may use at most 192 MiB of HBM per device.

v0:
```python
import jax
import jax.numpy as jnp
from jax import lax
from jax.sharding import PartitionSpec as P


def inner_product(first, second):
    return lax.dot_general(
        first,
        second,
        (((0,), (0,)), ((), ())),
        precision=lax.Precision.HIGHEST,
        preferred_element_type=jnp.float32,
    )


def plain_product(first, second):
    return jnp.dot(
        first, second, precision=lax.Precision.HIGHEST, preferred_element_type=jnp.float32
    )


def local(left_panel, right_panel, arc_basis, normal_block):
    left_count = left_panel.shape[0]
    right_count = right_panel.shape[0]
    col_index = lax.axis_index("col")
    row_index = lax.axis_index("row")
    basis_left = lax.dynamic_slice_in_dim(arc_basis, col_index * left_count, left_count, 0)
    basis_right = lax.dynamic_slice_in_dim(arc_basis, row_index * right_count, right_count, 0)
    left_coef = lax.psum(inner_product(basis_left, left_panel), "col")
    right_coef = lax.psum(inner_product(basis_right, right_panel), "row")
    left_reduced = left_panel - plain_product(basis_left, left_coef)
    right_reduced = right_panel - plain_product(basis_right, right_coef)
    initial = normal_block - inner_product(left_coef, right_coef)
    right_whole = lax.all_gather(right_panel, "row", axis=0, tiled=True)
    updated_block = initial + inner_product(
        lax.all_gather(left_panel, "col", axis=0, tiled=True), right_whole
    )
    return (updated_block, left_reduced, right_reduced)


def solution(mesh):
    in_specs = (P("col", "row"), P("row", "col"), P(), P("row", "col"))
    out_specs = (P("row", "col"), P("col", "row"), P("row", "col"))
    return jax.shard_map(local, mesh=mesh, in_specs=in_specs, out_specs=out_specs, check_vma=False)
```

profile of v0, /device:TPU:0, one launch (start us, length us, event | category | flops | bytes accessed | tf_op | source)
XLA Modules:
  0.0 972.1 jit_solution(14097927825804215923)
XLA Ops:
  7.2 0.0 all-reduce.3.cloned.1.call-start
  7.2 7.3 fusion.4
  14.5 0.0 all-reduce.3.cloned.1.call-update
  14.6 0.0 all-reduce.5.cloned.1.call-start
  14.6 10.7 %fusion.1 = f32[256,2048]{1,0:T(8,128)} fusion(f32[1024,2048]{1,0:T(8,128)} %param.5, f32[4096,256]{1,0:T(8,128)} %param.6, s32[]{:T(128)S(6)} %select_n.7), kind=kOutput, calls=%fused_computation.4 | convolution fusion | flops 6442450944 | bytes 11534340 | tf_op jit(solution)/shard_map/dot_general | solution.py:8
  25.3 0.0 all-reduce.5.cloned.1.call-update
  25.3 0.0 all-gather.5.cloned.1.call-start
  25.4 0.7 all-gather.5.cloned.1.call-update
  26.1 0.2 all-gather.3.cloned.1.call-start
  26.3 0.3 all-gather.3.cloned.1.call-update
  26.7 55.9 %all-reduce.3.cloned.1.call-done = f32[256,2048]{1,0:T(8,128)} async-done(((f32[256,2048]{1,0:T(8,128)}), f32[256,2048]{1,0:T(8,128)}) %all-reduce.3.cloned.1.call-update) | async-done | bytes 2097168 | tf_op jit(solution)/shard_map/psum | solution.py:30
  82.6 8.5 convolution_subtract_fusion.1
  91.1 0.0 copy-start
  91.1 64.3 %all-reduce.5.cloned.1.call-done = f32[256,2048]{1,0:T(8,128)} async-done(((f32[256,2048]{1,0:T(8,128)}), f32[256,2048]{1,0:T(8,128)}) %all-reduce.5.cloned.1.call-update) | async-done | bytes 2097168 | tf_op jit(solution)/shard_map/psum | solution.py:31
  155.4 0.0 copy-start.1
  155.4 13.3 %convolution_subtract_fusion = f32[1024,2048]{1,0:T(8,128)} fusion(f32[1024,2048]{1,0:T(8,128)} %param.5, f32[256,2048]{1,0:T(8,128)} %all-reduce.5.cloned.1.call-done, f32[4096,256]{1,0:T(8,128)} %param.6, s32[]{:T(128)S(6)} %select_n.7), kind=kOutput, calls=%fused_computation.1 | convolution fusion | flops 6444548096 | bytes 19922948 | tf_op jit(solution)/shard_map/dot_general | solution.py:18
  168.7 0.0 copy-done
  168.7 0.0 copy-done.1
  168.7 16.0 %fusion.10 = f32[2048,2048]{1,0:T(8,128)} fusion(f32[256,2048]{1,0:T(8,128)S(1)} %copy-done, f32[256,2048]{1,0:T(8,128)S(1)} %copy-done.1), kind=kOutput, calls=%fused_computation.13 | convolution fusion | flops 12884901888 | bytes 20971520 | tf_op jit(solution)/shard_map/dot_general | solution.py:8
  184.7 269.6 %all-gather.5.cloned.1.call-done = f32[4096,2048]{1,0:T(8,128)} async-done(((f32[1024,2048]{1,0:T(8,128)}), f32[4096,2048]{1,0:T(8,128)}) %all-gather.5.cloned.1.call-update) | async-done | bytes 33554448 | tf_op jit(solution)/shard_map/all_gather | solution.py:35
  454.3 290.1 %all-gather.3.cloned.1.call-done = f32[4096,2048]{1,0:T(8,128)} async-done(((f32[512,2048]{1,0:T(8,128)}), f32[4096,2048]{1,0:T(8,128)}) %all-gather.3.cloned.1.call-update) | async-done | bytes 33554448 | tf_op jit(solution)/shard_map/all_gather | solution.py:37
  744.4 221.2 %subtract_add_fusion = f32[2048,2048]{1,0:T(8,128)} fusion(f32[2048,2048]{1,0:T(8,128)} %param.7, f32[2048,2048]{1,0:T(8,128)} %fusion.10, f32[4096,2048]{1,0:T(8,128)} %all-gather.3.cloned.1.call-done, f32[4096,2048]{1,0:T(8,128)} %all-gather.5.cloned.1.call-done), kind=kOutput, calls=%fused_computation | convolution fusion | flops 206166818816 | bytes 117440512 | tf_op jit(solution)/shard_map/dot_general | solution.py:8
Async XLA Ops:
  7.2 75.4 %all-reduce.3.cloned.1.call-start = ((), (), s32[]{:S(2)}) async-start(), calls=%async_computation | async-start | bytes 4194304 | tf_op jit(solution)/shard_map/psum | solution.py:30
  14.6 140.8 %all-reduce.5.cloned.1.call-start = ((), (), s32[]{:S(2)}) async-start(), calls=%async_computation.1 | async-start | bytes 4194304 | tf_op jit(solution)/shard_map/psum | solution.py:31
  25.3 429.0 %all-gather.5.cloned.1.call-start = ((), (), s32[]{:S(2)}) async-start(), calls=%async_computation.3 | async-start | bytes 41943040 | tf_op jit(solution)/shard_map/all_gather | solution.py:35
  26.1 718.4 %all-gather.3.cloned.1.call-start = ((), (), s32[]{:S(2)}) async-start(), calls=%async_computation.2 | async-start | bytes 37748736 | tf_op jit(solution)/shard_map/all_gather | solution.py:37
  91.1 77.5 %copy-start = (f32[256,2048]{1,0:T(8,128)S(1)}, f32[256,2048]{1,0:T(8,128)}, u32[]{:S(2)}) copy-start(f32[256,2048]{1,0:T(8,128)} %all-reduce.3.cloned.1.call-done) | copy-start | bytes 6291460
  155.4 13.3 %copy-start.1 = (f32[256,2048]{1,0:T(8,128)S(1)}, f32[256,2048]{1,0:T(8,128)}, u32[]{:S(2)}) copy-start(f32[256,2048]{1,0:T(8,128)} %all-reduce.5.cloned.1.call-done) | copy-start | bytes 6291460
Sparse Core Ops, SparseCore 0:
  14.7 67.8 all-reduce.2
  86.3 69.0 all-reduce.4
  157.2 297.0 all-gather.4
  455.8 288.5 all-gather.2
where the time goes:
time: 972 us
  waiting for transfers between devices  681 us (70%)
  matrix products  277 us (28%)
  between operations  13.8 us (1%)
    all_gather x1, waiting for transfers between devices, local(): lax.all_gather(left_panel, 'col', axis=0, tiled=True)  290 us
    all_gather x1, waiting for transfers between devices, local(): right_whole = lax.all_gather(right_panel, 'row', axis=0, tiled=True)  270 us
    dot_general x4, matrix products, inner_product(): lax.dot_general(first, second, (((0,), (0,)), ((), ())), precision=lax.Pr...  255 us
    psum x1, waiting for transfers between devices, local(): right_coef = lax.psum(inner_product(basis_right, right_panel), 'row')  64.3 us
    psum x1, waiting for transfers between devices, local(): left_coef = lax.psum(inner_product(basis_left, left_panel), 'col')  55.9 us
    dot_general x2, matrix products, plain_product(): jnp.dot(first, second, precision=lax.Precision.HIGHEST, preferred_element...  21.8 us
  transfers between devices with their start and end apart: 4, of which 4 were waited for; matrix products, arithmetic and copies ran while one was open for 5% of the time, Pallas kernels for 0%

commit v1 on v0

v1 whole, which is shorter than its diff:
```python
import functools

import jax
import jax.numpy as jnp
from jax import lax
from jax.sharding import PartitionSpec as P


def inner_product(first, second):
    return lax.dot_general(
        first,
        second,
        (((0,), (0,)), ((), ())),
        precision=lax.Precision.HIGH,
        preferred_element_type=jnp.float32,
    )


def plain_product(first, second):
    return jnp.dot(
        first, second, precision=lax.Precision.HIGH, preferred_element_type=jnp.float32
    )


def shift(block, axis, size, distance):
    return lax.ppermute(block, axis, [(i, i ^ distance) for i in range(size)])


def gather_right(owns, rows, row_index):
    if rows != 4:
        return [lax.all_gather(own, "row", axis=0, tiled=True) for own in owns]
    count = owns[0].shape[0]
    half = count // 2
    firsts, seconds, wholes = [], [], []
    for phase, own in enumerate(owns):
        if phase >= 2:
            own, firsts[phase - 2], seconds[phase - 2] = lax.optimization_barrier(
                (own, firsts[phase - 2], seconds[phase - 2])
            )
        firsts.append(shift(own, "row", rows, 1))
        seconds.append(shift(own, "row", rows, 2))
    for own, first, second in zip(owns, firsts, seconds):
        third_top = shift(first[:half], "row", rows, 2)
        third_bottom = shift(second[half:], "row", rows, 1)
        whole = jnp.zeros((rows * count, own.shape[1]), own.dtype)
        for piece, distance, offset in (
            (own, 0, 0),
            (first, 1, 0),
            (second, 2, 0),
            (third_top, 3, 0),
            (third_bottom, 3, half),
        ):
            start = (row_index ^ distance) * count + offset
            whole = lax.dynamic_update_slice_in_dim(whole, piece, start, 0)
        wholes.append(whole)
    return wholes


def local(rows, cols, phases, left_panel, right_panel, arc_basis, normal_block):
    left_count = left_panel.shape[0]
    right_count = right_panel.shape[0]
    per = left_count // phases
    ratio = right_count // left_count
    col_index = lax.axis_index("col")
    row_index = lax.axis_index("row")
    right_split = right_panel.reshape(ratio, left_count, -1)
    basis_split = arc_basis.reshape(cols, left_count, -1)
    spans = [slice(phase * per, (phase + 1) * per) for phase in range(phases)]
    owns = [right_split[:, span].reshape(ratio * per, -1) for span in spans]
    bases = [basis_split[:, span].reshape(cols * per, -1) for span in spans]
    lefts = []
    for span in spans:
        lefts.append(lax.all_gather(left_panel[span], "col", axis=0, tiled=True))
    rights = gather_right(owns, rows, row_index)
    block = normal_block
    left_coef = 0.0
    right_coef = 0.0
    for left, right, basis in zip(lefts, rights, bases):
        right_coef = right_coef + inner_product(basis, right)
        left_coef = left_coef + inner_product(basis, left)
        block = block + inner_product(left, right)
        block, left_coef, right_coef = lax.optimization_barrier(
            (block, left_coef, right_coef)
        )
    basis_left = lax.dynamic_slice_in_dim(arc_basis, col_index * left_count, left_count, 0)
    basis_right = lax.dynamic_slice_in_dim(arc_basis, row_index * right_count, right_count, 0)
    left_reduced = left_panel - plain_product(basis_left, left_coef)
    right_reduced = right_panel - plain_product(basis_right, right_coef)
    updated_block = block - inner_product(left_coef, right_coef)
    return (updated_block, left_reduced, right_reduced)


def solution(mesh):
    rows, cols = mesh.shape["row"], mesh.shape["col"]
    in_specs = (P("col", "row"), P("row", "col"), P(), P("row", "col"))
    out_specs = (P("row", "col"), P("col", "row"), P("row", "col"))
    phases = 4
    return jax.shard_map(
        functools.partial(local, rows, cols, phases),
        mesh=mesh,
        in_specs=in_specs,
        out_specs=out_specs,
        check_vma=False,
    )
```

time: 972 us -> 559 us (0.58); the launches traced: 972 us -> 548 us
  waiting for transfers between devices: 681 us -> 174 us
  local copies, waits for them, and re-layouts: 0.01 us -> 89.4 us
  matrix products: 277 us -> 237 us
  starting transfers between devices: 0.34 us -> 21.7 us
  other arithmetic: 0 us -> 9.93 us
    all_gather x2 -> x4, waiting for transfers between devices: 560 us -> 0.01 us  [local(): lefts.append(lax.all_gather(left_panel[span], 'col', axis=0, tiled=True))]
    ppermute x0 -> x16, waiting for transfers between devices: none -> 173 us  [shift(): return lax.ppermute(block, axis, [(i, i ^ distance) for i in range(size)])]
    psum x2 -> x0, waiting for transfers between devices: 120 us -> none  [the longest x1 64.3 us: local(): right_coef = lax.psum(inner_product(basis_right, right_panel), 'row')]
    unnamed x4 -> x48, local copies, waits for them, and re-layouts: 0.01 us -> 35.6 us
    dot_general x4 -> x13, matrix products: 255 us -> 221 us  [inner_product(): lax.dot_general(first, second, (((0,), (0,)), ((), ())), precision=lax.Pr...]
    slice x0 -> x11, local copies, waits for them, and re-layouts: none -> 26.8 us  [the longest x4 7.34 us: gather_right(): third_top = shift(first[:half], 'row', rows, 2)]
    dynamic_update_slice x0 -> x20, local copies, waits for them, and re-layouts: none -> 22.9 us  [gather_right(): whole = lax.dynamic_update_slice_in_dim(whole, piece, start, 0)]
    ppermute x0 -> x16, starting transfers between devices: none -> 21.5 us  [shift(): return lax.ppermute(block, axis, [(i, i ^ distance) for i in range(size)])]
  transfers between devices with their start and end apart: 4 -> 20, of which waited for: 4 -> 10; matrix products, arithmetic and copies ran while one was open for 5% -> 44% of each run, Pallas kernels for 0% -> 0%
where the time goes in v1:
time: 559 us; the launch traced here: 548 us
  matrix products  237 us (42%)
  waiting for transfers between devices  174 us (31%)
  local copies, waits for them, and re-layouts  89.4 us (16%)
  starting transfers between devices  21.7 us (4%)
  between operations  14.7 us (3%)
  other arithmetic  9.93 us (2%)
    dot_general x13, matrix products, inner_product(): lax.dot_general(first, second, (((0,), (0,)), ((), ())), precision=lax.Pr...  221 us
    ppermute x16, waiting for transfers between devices, shift(): return lax.ppermute(block, axis, [(i, i ^ distance) for i in range(size)])  173 us
    unnamed x48, local copies, waits for them, and re-layouts  35.6 us
    dynamic_update_slice x20, local copies, waits for them, and re-layouts, gather_right(): whole = lax.dynamic_update_slice_in_dim(whole, piece, start, 0)  22.9 us
    ppermute x16, starting transfers between devices, shift(): return lax.ppermute(block, axis, [(i, i ^ distance) for i in range(size)])  21.5 us
    dot_general x2, matrix products, plain_product(): jnp.dot(first, second, precision=lax.Precision.HIGH, preferred_element_ty...  16.4 us
  transfers between devices with their start and end apart: 20, of which 10 were waited for; matrix products, arithmetic and copies ran while one was open for 44% of the time, Pallas kernels for 0%

profile of v1, /device:TPU:0, one launch (start us, length us, event | category | flops | bytes accessed | tf_op | source)
XLA Modules:
  0.0 547.6 jit_solution(13097727572962516773)
XLA Ops:
  7.2 4.3 fusion.6
  13.1 7.1 %fusion.4 = (f32[2,128,2048]{2,1,0:T(8,128)}, f32[2,128,2048]{2,1,0:T(8,128)}, f32[2,128,2048]{2,1,0:T(8,128)}, f32[2,128,2048]{2,1,0:T(8,128)}) fusion(f32[2,512,2048]{2,1,0:T(8,128)} %bitcast.54), kind=kLoop, calls=%fused_computation.35 | loop fusion | bytes 16777216 | tf_op jit(solution)/shard_map/slice | solution.py:69
  20.2 3.0 collective-permute-start.4
  25.3 17.7 %copy.7 = f32[2048,2048]{0,1:T(8,128)} copy(f32[2048,2048]{1,0:T(8,128)} %param.7) | data formatting | bytes 33554432 | tf_op args[3]
  53.5 16.4 %collective-permute-done.4 = f32[256,2048]{1,0:T(8,128)} collective-permute-done((f32[256,2048]{1,0:T(8,128)}, f32[256,2048]{1,0:T(8,128)}, u32[]{:S(2)}, u32[]{:S(2)}) %collective-permute-start.4) | collective-permute-done | bytes 2097184 | tf_op jit(solution)/shard_map/ppermute | solution.py:26
  72.0 2.3 slice.68
  75.8 2.3 slice.69
  78.7 36.2 %collective-permute-done = f32[256,2048]{1,0:T(8,128)} collective-permute-done((f32[256,2048]{1,0:T(8,128)}, f32[256,2048]{1,0:T(8,128)}, u32[]{:S(2)}, u32[]{:S(2)}) %collective-permute-start) | collective-permute-done | bytes 2097184 | tf_op jit(solution)/shard_map/ppermute | solution.py:26
  117.0 2.4 slice.62
  132.7 6.7 %collective-permute-done.6 = f32[128,2048]{1,0:T(8,128)S(1)} collective-permute-done((f32[128,2048]{1,0:T(8,128)}, f32[128,2048]{1,0:T(8,128)S(1)}, u32[]{:S(2)}, u32[]{:S(2)}) %collective-permute-start.6) | collective-permute-done | bytes 1048608 | tf_op jit(solution)/shard_map/ppermute | solution.py:26
  141.4 20.4 %collective-permute-done.2 = f32[128,2048]{1,0:T(8,128)S(1)} collective-permute-done((f32[128,2048]{1,0:T(8,128)}, f32[128,2048]{1,0:T(8,128)S(1)}, u32[]{:S(2)}, u32[]{:S(2)}) %collective-permute-start.2) | collective-permute-done | bytes 1048608 | tf_op jit(solution)/shard_map/ppermute | solution.py:26
  165.6 10.3 %convolution_bitcast_fusion.2 = f32[256,2048]{0,1:T(8,128)} fusion(f32[1024,2048]{1,0:T(8,128)S(1)} %constant_dynamic-update-slice_fusion.10, f32[1024,256]{1,0:T(8,128)} %bitcast.59), kind=kOutput, calls=%fused_computation.9 | convolution fusion | flops 3221225472 | bytes 11534336 | tf_op jit(solution)/shard_map/dot_general | solution.py:10
  175.9 9.9 %convolution_bitcast_fusion.3 = f32[256,2048]{0,1:T(8,128)} fusion(f32[1024,2048]{1,0:T(8,128)S(1)} %constant_dynamic-update-slice_fusion.15, f32[1024,256]{1,0:T(8,128)} %bitcast.61), kind=kOutput, calls=%fused_computation.10 | convolution fusion | flops 3221225472 | bytes 11534336 | tf_op jit(solution)/shard_map/dot_general | solution.py:10
  185.8 19.0 %collective-permute-done.8 = f32[256,2048]{1,0:T(8,128)} collective-permute-done((f32[256,2048]{1,0:T(8,128)}, f32[256,2048]{1,0:T(8,128)}, u32[]{:S(2)}, u32[]{:S(2)}) %collective-permute-start.8) | collective-permute-done | bytes 2097184 | tf_op jit(solution)/shard_map/ppermute | solution.py:26
  211.1 38.6 %collective-permute-done.12 = f32[256,2048]{1,0:T(8,128)} collective-permute-done((f32[256,2048]{1,0:T(8,128)}, f32[256,2048]{1,0:T(8,128)}, u32[]{:S(2)}, u32[]{:S(2)}) %collective-permute-start.12) | collective-permute-done | bytes 2097184 | tf_op jit(solution)/shard_map/ppermute | solution.py:26
  251.1 2.1 collective-permute-start.14
  263.4 10.7 %collective-permute-done.10 = f32[128,2048]{1,0:T(8,128)S(1)} collective-permute-done((f32[128,2048]{1,0:T(8,128)S(1)}, f32[128,2048]{1,0:T(8,128)S(1)}, u32[]{:S(2)}, u32[]{:S(2)}) %collective-permute-start.10) | collective-permute-done | bytes 1048608 | tf_op jit(solution)/shard_map/ppermute | solution.py:26
  274.4 20.8 %collective-permute-done.14 = f32[128,2048]{1,0:T(8,128)S(1)} collective-permute-done((f32[128,2048]{1,0:T(8,128)S(1)}, f32[128,2048]{1,0:T(8,128)S(1)}, u32[]{:S(2)}, u32[]{:S(2)}) %collective-permute-start.14) | collective-permute-done | bytes 1048608 | tf_op jit(solution)/shard_map/ppermute | solution.py:26
  295.5 8.5 %convolution_bitcast_fusion.1 = f32[256,2048]{0,1:T(8,128)} fusion(f32[1024,2048]{1,0:T(8,128)S(1)} %constant_dynamic-update-slice_fusion.5, f32[1024,256]{1,0:T(8,128)S(1)} %bitcast.57), kind=kOutput, calls=%fused_computation.8 | convolution fusion | flops 3221225472 | bytes 11534336 | tf_op jit(solution)/shard_map/dot_general | solution.py:10
  304.0 8.3 %convolution_bitcast_fusion = f32[256,2048]{0,1:T(8,128)} fusion(f32[1024,2048]{1,0:T(8,128)S(1)} %constant_dynamic-update-slice_fusion, f32[1024,256]{1,0:T(8,128)S(1)} %bitcast.55), kind=kOutput, calls=%fused_computation.7 | convolution fusion | flops 3221225472 | bytes 11534336 | tf_op jit(solution)/shard_map/dot_general | solution.py:10
  312.3 8.4 %fusion.7 = f32[256,2048]{1,0:T(8,128)} fusion(f32[1024,256]{1,0:T(8,128)S(1)} %bitcast.62, f32[1024,2048]{1,0:T(8,128)} %all-gather.5.cloned.1.call-done), kind=kOutput, calls=%fused_computation.38 | convolution fusion | flops 3221225472 | bytes 11534336 | tf_op jit(solution)/shard_map/dot_general | solution.py:10
  320.7 35.7 %bitcast_add_fusion.3 = f32[2048,2048]{0,1:T(8,128)} fusion(f32[2048,2048]{0,1:T(8,128)} %copy.7, f32[1024,2048]{1,0:T(8,128)} %copy-done.2, f32[1024,2048]{1,0:T(8,128)S(1)} %copy-done.15), kind=kOutput, calls=%fused_computation.3 | convolution fusion | flops 25773998080 | bytes 50331648 | tf_op jit(solution)/shard_map/dot_general | solution.py:10
  358.0 6.3 %fusion.8 = f32[256,2048]{1,0:T(8,128)S(1)} fusion(f32[1024,256]{1,0:T(8,128)S(1)} %bitcast.60, f32[1024,2048]{1,0:T(8,128)} %all-gather.7.cloned.1.call-done), kind=kOutput, calls=%fused_computation.39 | convolution fusion | flops 3221225472 | bytes 11534336 | tf_op jit(solution)/shard_map/dot_general | solution.py:10
  365.9 36.0 %bitcast_add_fusion.2 = f32[2048,2048]{0,1:T(8,128)} fusion(f32[2048,2048]{0,1:T(8,128)} %bitcast_add_fusion.3, f32[1024,2048]{1,0:T(8,128)} %copy-done.1, f32[1024,2048]{1,0:T(8,128)S(1)} %copy-done.14), kind=kOutput, calls=%fused_computation.2 | convolution fusion | flops 25773998080 | bytes 50331648 | tf_op jit(solution)/shard_map/dot_general | solution.py:10
  403.5 6.3 %fusion.9 = f32[256,2048]{1,0:T(8,128)S(1)} fusion(f32[1024,256]{1,0:T(8,128)S(1)} %bitcast.58, f32[1024,2048]{1,0:T(8,128)} %all-gather.9.cloned.1.call-done), kind=kOutput, calls=%fused_computation.40 | convolution fusion | flops 3221225472 | bytes 11534336 | tf_op jit(solution)/shard_map/dot_general | solution.py:10
  411.4 35.7 %bitcast_add_fusion.1 = f32[2048,2048]{0,1:T(8,128)} fusion(f32[2048,2048]{0,1:T(8,128)} %bitcast_add_fusion.2, f32[1024,2048]{1,0:T(8,128)} %copy-done.3, f32[1024,2048]{1,0:T(8,128)S(1)} %copy-done.13), kind=kOutput, calls=%fused_computation.1 | convolution fusion | flops 25773998080 | bytes 50331648 | tf_op jit(solution)/shard_map/dot_general | solution.py:10
  448.7 6.4 %fusion.10 = f32[256,2048]{1,0:T(8,128)S(1)} fusion(f32[1024,256]{1,0:T(8,128)S(1)} %bitcast.56, f32[1024,2048]{1,0:T(8,128)} %all-gather.11.cloned.1.call-done), kind=kOutput, calls=%fused_computation.41 | convolution fusion | flops 3221225472 | bytes 11534336 | tf_op jit(solution)/shard_map/dot_general | solution.py:10
  457.0 35.7 %bitcast_add_fusion = f32[2048,2048]{0,1:T(8,128)} fusion(f32[2048,2048]{0,1:T(8,128)} %bitcast_add_fusion.1, f32[1024,2048]{1,0:T(8,128)} %copy-done, f32[1024,2048]{1,0:T(8,128)S(1)} %copy-done.16), kind=kOutput, calls=%fused_computation | convolution fusion | flops 25773998080 | bytes 50331648 | tf_op jit(solution)/shard_map/dot_general | solution.py:10
  492.7 13.7 %convolution_subtract_fusion = f32[2048,2048]{0,1:T(8,128)} fusion(f32[2048,2048]{0,1:T(8,128)} %bitcast_add_fusion, f32[256,2048]{1,0:T(8,128)S(1)} %add.88, f32[256,2048]{0,1:T(8,128)S(1)} %copy-done.4), kind=kOutput, calls=%fused_computation.4 | convolution fusion | flops 6446645248 | bytes 37748736 | tf_op jit(solution)/shard_map/dot_general | solution.py:10
  506.4 17.8 %copy.9 = f32[2048,2048]{1,0:T(8,128)} copy(f32[2048,2048]{0,1:T(8,128)} %convolution_subtract_fusion) | data formatting | bytes 33554432
  524.2 11.4 %convolution_subtract_fusion.1 = f32[1024,2048]{1,0:T(8,128)} fusion(f32[1024,2048]{1,0:T(8,128)} %param.5, f32[256,2048]{0,1:T(8,128)} %add.89, f32[4096,256]{1,0:T(8,128)} %param.6, s32[]{:T(128)S(6)} %select_n.20), kind=kOutput, calls=%fused_computation.5 | convolution fusion | flops 3223322624 | bytes 19922948 | tf_op jit(solution)/shard_map/dot_general | solution.py:20
  535.6 5.1 convolution_subtract_fusion.2
  (116 shorter events, 67.5 us)
Async XLA Ops:
  7.2 305.2 %all-gather.5.cloned.1.call-start = ((), (), s32[]{:S(2)}) async-start(), calls=%async_computation | async-start | bytes 9437184 | tf_op jit(solution)/shard_map/all_gather | solution.py:73
  11.6 346.5 %all-gather.7.cloned.1.call-start = ((), (), s32[]{:S(2)}) async-start(), calls=%async_computation.1 | async-start | bytes 9437184 | tf_op jit(solution)/shard_map/all_gather | solution.py:73
  12.3 391.2 %all-gather.9.cloned.1.call-start = ((), (), s32[]{:S(2)}) async-start(), calls=%async_computation.2 | async-start | bytes 9437184 | tf_op jit(solution)/shard_map/all_gather | solution.py:73
  13.0 435.7 %all-gather.11.cloned.1.call-start = ((), (), s32[]{:S(2)}) async-start(), calls=%async_computation.3 | async-start | bytes 9437184 | tf_op jit(solution)/shard_map/all_gather | solution.py:73
  20.2 49.8 %collective-permute-start.4 = (f32[256,2048]{1,0:T(8,128)}, f32[256,2048]{1,0:T(8,128)}, u32[]{:S(2)}, u32[]{:S(2)}) collective-permute-start(f32[256,2048]{1,0:T(8,128)} %bitcast.7), channel_id=1, source_target_pairs={{0,8},{8,0},{16,24},{24,16},{1,9},{9,1},{17,25},{25,17},{2,10},{10... | collective-permute-start | bytes 6291464 | tf_op jit(solution)/shard_map/ppermute | solution.py:26
  23.2 48.8 %collective-permute-start.5 = (f32[256,2048]{1,0:T(8,128)}, f32[256,2048]{1,0:T(8,128)}, u32[]{:S(2)}, u32[]{:S(2)}) collective-permute-start(f32[256,2048]{1,0:T(8,128)} %bitcast.7), channel_id=1, source_target_pairs={{0,16},{8,24},{16,0},{24,8},{1,17},{9,25},{17,1},{25,9},{2,18},{10... | collective-permute-start | bytes 6291464 | tf_op jit(solution)/shard_map/ppermute | solution.py:26
  24.7 90.2 %collective-permute-start = (f32[256,2048]{1,0:T(8,128)}, f32[256,2048]{1,0:T(8,128)}, u32[]{:S(2)}, u32[]{:S(2)}) collective-permute-start(f32[256,2048]{1,0:T(8,128)} %bitcast.1), channel_id=1, source_target_pairs={{0,8},{8,0},{16,24},{24,16},{1,9},{9,1},{17,25},{25,17},{2,10},{10... | collective-permute-start | bytes 6291464 | tf_op jit(solution)/shard_map/ppermute | solution.py:26
  25.3 91.7 %collective-permute-start.1 = (f32[256,2048]{1,0:T(8,128)}, f32[256,2048]{1,0:T(8,128)}, u32[]{:S(2)}, u32[]{:S(2)}) collective-permute-start(f32[256,2048]{1,0:T(8,128)} %bitcast.1), channel_id=1, source_target_pairs={{0,16},{8,24},{16,0},{24,8},{1,17},{9,25},{17,1},{25,9},{2,18},{10... | collective-permute-start | bytes 6291464 | tf_op jit(solution)/shard_map/ppermute | solution.py:26
  74.3 65.0 %collective-permute-start.6 = (f32[128,2048]{1,0:T(8,128)}, f32[128,2048]{1,0:T(8,128)S(1)}, u32[]{:S(2)}, u32[]{:S(2)}) collective-permute-start(f32[128,2048]{1,0:T(8,128)} %slice.68), channel_id=1, source_target_pairs={{0,16},{8,24},{16,0},{24,8},{1,17},{9,25},{17,1},{25,9},{2,18},{10... | collective-permute-start | bytes 3145736 | tf_op jit(solution)/shard_map/ppermute | solution.py:26
  78.1 62.7 %collective-permute-start.7 = (f32[128,2048]{1,0:T(8,128)}, f32[128,2048]{1,0:T(8,128)S(1)}, u32[]{:S(2)}, u32[]{:S(2)}) collective-permute-start(f32[128,2048]{1,0:T(8,128)} %slice.69), channel_id=1, source_target_pairs={{0,8},{8,0},{16,24},{24,16},{1,9},{9,1},{17,25},{25,17},{2,10},{10... | collective-permute-start | bytes 3145736 | tf_op jit(solution)/shard_map/ppermute | solution.py:26
  119.3 42.5 %collective-permute-start.2 = (f32[128,2048]{1,0:T(8,128)}, f32[128,2048]{1,0:T(8,128)S(1)}, u32[]{:S(2)}, u32[]{:S(2)}) collective-permute-start(f32[128,2048]{1,0:T(8,128)} %slice.62), channel_id=1, source_target_pairs={{0,16},{8,24},{16,0},{24,8},{1,17},{9,25},{17,1},{25,9},{2,18},{10... | collective-permute-start | bytes 3145736 | tf_op jit(solution)/shard_map/ppermute | solution.py:26
  125.0 40.4 %collective-permute-start.3 = (f32[128,2048]{1,0:T(8,128)S(1)}, f32[128,2048]{1,0:T(8,128)S(1)}, u32[]{:S(2)}, u32[]{:S(2)}) collective-permute-start(f32[128,2048]{1,0:T(8,128)S(1)} %slice.63), channel_id=1, source_target_pairs={{0,8},{8,0},{16,24},{24,16},{1,9},{9,1},{17,25},{25,17},{2,10},{10... | collective-permute-start | bytes 3145736 | tf_op jit(solution)/shard_map/ppermute | solution.py:26
  125.6 79.2 %collective-permute-start.8 = (f32[256,2048]{1,0:T(8,128)}, f32[256,2048]{1,0:T(8,128)}, u32[]{:S(2)}, u32[]{:S(2)}) collective-permute-start(f32[256,2048]{1,0:T(8,128)} %bitcast.2), channel_id=1, source_target_pairs={{0,8},{8,0},{16,24},{24,16},{1,9},{9,1},{17,25},{25,17},{2,10},{10... | collective-permute-start | bytes 6291464 | tf_op jit(solution)/shard_map/ppermute | solution.py:26
  139.3 68.9 %collective-permute-start.9 = (f32[256,2048]{1,0:T(8,128)}, f32[256,2048]{1,0:T(8,128)}, u32[]{:S(2)}, u32[]{:S(2)}) collective-permute-start(f32[256,2048]{1,0:T(8,128)} %bitcast.2), channel_id=1, source_target_pairs={{0,16},{8,24},{16,0},{24,8},{1,17},{9,25},{17,1},{25,9},{2,18},{10... | collective-permute-start | bytes 6291464 | tf_op jit(solution)/shard_map/ppermute | solution.py:26
  140.8 108.9 %collective-permute-start.12 = (f32[256,2048]{1,0:T(8,128)}, f32[256,2048]{1,0:T(8,128)}, u32[]{:S(2)}, u32[]{:S(2)}) collective-permute-start(f32[256,2048]{1,0:T(8,128)} %bitcast.8), channel_id=1, source_target_pairs={{0,8},{8,0},{16,24},{24,16},{1,9},{9,1},{17,25},{25,17},{2,10},{10... | collective-permute-start | bytes 6291464 | tf_op jit(solution)/shard_map/ppermute | solution.py:26
  161.8 91.4 %collective-permute-start.13 = (f32[256,2048]{1,0:T(8,128)}, f32[256,2048]{1,0:T(8,128)}, u32[]{:S(2)}, u32[]{:S(2)}) collective-permute-start(f32[256,2048]{1,0:T(8,128)} %bitcast.8), channel_id=1, source_target_pairs={{0,16},{8,24},{16,0},{24,8},{1,17},{9,25},{17,1},{25,9},{2,18},{10... | collective-permute-start | bytes 6291464 | tf_op jit(solution)/shard_map/ppermute | solution.py:26
  165.5 20.3 %copy-start.1 = (f32[1024,2048]{1,0:T(8,128)}, f32[1024,2048]{1,0:T(8,128)S(1)}, u32[]{:S(2)}) copy-start(f32[1024,2048]{1,0:T(8,128)S(1)} %constant_dynamic-update-slice_fusion.10) | copy-start | bytes 25165828
  206.2 68.0 %collective-permute-start.10 = (f32[128,2048]{1,0:T(8,128)S(1)}, f32[128,2048]{1,0:T(8,128)S(1)}, u32[]{:S(2)}, u32[]{:S(2)}) collective-permute-start(f32[128,2048]{1,0:T(8,128)S(1)} %slice.86), channel_id=1, source_target_pairs={{0,16},{8,24},{16,0},{24,8},{1,17},{9,25},{17,1},{25,9},{2,18},{10... | collective-permute-start | bytes 3145736 | tf_op jit(solution)/shard_map/ppermute | solution.py:26
  209.6 64.7 %collective-permute-start.11 = (f32[128,2048]{1,0:T(8,128)S(1)}, f32[128,2048]{1,0:T(8,128)S(1)}, u32[]{:S(2)}, u32[]{:S(2)}) collective-permute-start(f32[128,2048]{1,0:T(8,128)S(1)} %slice.87), channel_id=1, source_target_pairs={{0,8},{8,0},{16,24},{24,16},{1,9},{9,1},{17,25},{25,17},{2,10},{10... | collective-permute-start | bytes 3145736 | tf_op jit(solution)/shard_map/ppermute | solution.py:26
  251.1 44.1 %collective-permute-start.14 = (f32[128,2048]{1,0:T(8,128)S(1)}, f32[128,2048]{1,0:T(8,128)S(1)}, u32[]{:S(2)}, u32[]{:S(2)}) collective-permute-start(f32[128,2048]{1,0:T(8,128)S(1)} %slice.89), channel_id=1, source_target_pairs={{0,16},{8,24},{16,0},{24,8},{1,17},{9,25},{17,1},{25,9},{2,18},{10... | collective-permute-start | bytes 3145736 | tf_op jit(solution)/shard_map/ppermute | solution.py:26
  254.5 40.8 %collective-permute-start.15 = (f32[128,2048]{1,0:T(8,128)S(1)}, f32[128,2048]{1,0:T(8,128)S(1)}, u32[]{:S(2)}, u32[]{:S(2)}) collective-permute-start(f32[128,2048]{1,0:T(8,128)S(1)} %slice.90), channel_id=1, source_target_pairs={{0,8},{8,0},{16,24},{24,16},{1,9},{9,1},{17,25},{25,17},{2,10},{10... | collective-permute-start | bytes 3145736 | tf_op jit(solution)/shard_map/ppermute | solution.py:26
  259.7 35.8 %copy-start.6 = (f32[8,128,256]{2,1,0:T(8,128)S(1)}, f32[8,128,256]{2,1,0:T(8,128)}, u32[]{:S(2)}) copy-start(f32[8,128,256]{2,1,0:T(8,128)} %get-tuple-element.47) | copy-start | bytes 3145732
  274.4 21.1 %copy-start.3 = (f32[1024,2048]{1,0:T(8,128)}, f32[1024,2048]{1,0:T(8,128)S(1)}, u32[]{:S(2)}) copy-start(f32[1024,2048]{1,0:T(8,128)S(1)} %constant_dynamic-update-slice_fusion.5) | copy-start | bytes 25165828
  320.7 35.7 %copy-start.17 = (f32[256,2048]{0,1:T(8,128)S(1)}, f32[256,2048]{0,1:T(8,128)}, u32[]{:S(2)}) copy-start(f32[256,2048]{0,1:T(8,128)} %convolution_bitcast_fusion.2) | copy-start | bytes 6291460
  320.7 35.7 %copy-start.18 = (f32[256,2048]{0,1:T(8,128)S(1)}, f32[256,2048]{0,1:T(8,128)}, u32[]{:S(2)}) copy-start(f32[256,2048]{0,1:T(8,128)} %convolution_bitcast_fusion.3) | copy-start | bytes 6291460
  320.7 37.3 %copy-start.8 = (f32[8,128,256]{2,1,0:T(8,128)S(1)}, f32[8,128,256]{2,1,0:T(8,128)}, u32[]{:S(2)}) copy-start(f32[8,128,256]{2,1,0:T(8,128)} %get-tuple-element.48) | copy-start | bytes 3145732
  365.9 36.0 %copy-start.10 = (f32[256,2048]{0,1:T(8,128)S(1)}, f32[256,2048]{0,1:T(8,128)}, u32[]{:S(2)}) copy-start(f32[256,2048]{0,1:T(8,128)} %add.83) | copy-start | bytes 6291460
  365.9 36.0 %copy-start.20 = (f32[256,2048]{0,1:T(8,128)S(1)}, f32[256,2048]{0,1:T(8,128)}, u32[]{:S(2)}) copy-start(f32[256,2048]{0,1:T(8,128)} %convolution_bitcast_fusion.1) | copy-start | bytes 6291460
  365.9 37.6 %copy-start.7 = (f32[8,128,256]{2,1,0:T(8,128)S(1)}, f32[8,128,256]{2,1,0:T(8,128)}, u32[]{:S(2)}) copy-start(f32[8,128,256]{2,1,0:T(8,128)} %get-tuple-element.47) | copy-start | bytes 3145732
  411.4 35.7 %copy-start.11 = (f32[256,2048]{0,1:T(8,128)S(1)}, f32[256,2048]{0,1:T(8,128)}, u32[]{:S(2)}) copy-start(f32[256,2048]{0,1:T(8,128)} %add.86) | copy-start | bytes 6291460
  411.4 35.7 %copy-start.19 = (f32[256,2048]{0,1:T(8,128)S(1)}, f32[256,2048]{0,1:T(8,128)}, u32[]{:S(2)}) copy-start(f32[256,2048]{0,1:T(8,128)} %convolution_bitcast_fusion) | copy-start | bytes 6291460
  457.0 35.7 %copy-start.4 = (f32[256,2048]{0,1:T(8,128)S(1)}, f32[256,2048]{0,1:T(8,128)}, u32[]{:S(2)}) copy-start(f32[256,2048]{0,1:T(8,128)} %add.89) | copy-start | bytes 6291460
  (11 other events, 98.4 us)
Sparse Core Ops, SparseCore 0:
  11.7 84.7 all-gather.4
  98.1 80.5 all-gather.6
  180.2 80.5 all-gather.8
  262.2 80.5 all-gather.10
